TPU v7x, 32 devices: a whole 2x2x4 slice. The times are simulated.
32 devices in a mesh: slab: 8 (over y, x, core), grp: 4 (over z).
Axes of the slice: x: 2, y: 2, z: 4, core: 2. Of those that a mesh axis runs over, the one named last changes fastest.
Arguments:
- resid7: float32 [512, 4096], P(None, ('slab', 'grp')), may hold values from -6 to 6
- interp73: float32 [8, 4], replicated, may hold values from -2 to 2
- interp31: float32 [4, 2], replicated, may hold values from -4 to 4
- elem_ops: float32 [8, 8, 4096], P(None, None, 'slab'), as said below
- conn: int32 [8, 4096], P(None, 'slab'), may hold values from 0 to 1121, as said below
- faces: int32 [2, 8, 561], P(None, 'slab'), may hold values from 0 to 1121, as said below
Outputs:
- correction3: float32 [64, 4096], P(None, ('slab', 'grp'))
Inputs may be any that keep to these rules, and one draw needn't show every extreme that they name: `conn`: the 512 columns of a slab describe a block of 32 x 16 x 1 hexahedra stacked along the long direction; column e lists the corners of one element, the corner at offsets (i, j, k) along (long, second, first direction) in row 4 i + 2 j + k; the slab's nodes are numbered 0 to 1121 in some order and every one of them is a corner of some element. faces[0, s] lists the 561 nodes of slab s on its face toward slab s - 1, faces[1, s] those on its face toward slab s + 1, all distinct; faces[1, s, f] and faces[0, s + 1, f] are the same point of the mesh. `elem_ops`: each element's matrix is symmetric, and each diagonal entry is positive and larger than the sum of magnitudes of the other entries of its row.
All inputs are finite; a program needn't handle non-finite values.
Results may differ from a plain program's by a relative error of at most 0.0003.
Values sent between devices are 32-bit elements; how exact they have to be, the bound alone decides.
A program may use at most 64 MiB of HBM per device.

v0:
```python
import jax
import jax.numpy as jnp
from jax import lax
from jax.sharding import PartitionSpec as P

EX = 32
EY = 16
SWEEPS = 2
lam_low = 0.3
lam_high = 1.9


def extended(array, sides, width):
    for axis, dim in sides:
        count, length = (lax.axis_size(axis), array.shape[dim])
        up = [(i, (i + 1) % count) for i in range(count - 1)]
        down = [(j, i) for i, j in up]
        last = lax.slice_in_dim(array, length - width, length, axis=dim)
        first = lax.slice_in_dim(array, 0, width, axis=dim)
        before = lax.ppermute(last, axis, up)
        after = lax.ppermute(first, axis, down)
        array = jnp.concatenate([before, array, after], axis=dim)
    return array


def restrict_high(block, interp73):
    hi = lax.Precision.HIGHEST
    width = block.shape[1]
    cube = block.reshape(8, 8, 8, width)
    cube = jnp.einsum("kc,ijkm->ijcm", interp73, cube, precision=hi)
    cube = jnp.einsum("jb,ijcm->ibcm", interp73, cube, precision=hi)
    cube = jnp.einsum("ia,ibcm->abcm", interp73, cube, precision=hi)
    return cube.reshape(64, width)


def restrict_low(block, interp31):
    hi = lax.Precision.HIGHEST
    width = block.shape[1]
    cube = block.reshape(4, 4, 4, width)
    cube = jnp.einsum("kc,ijkm->ijcm", interp31, cube, precision=hi)
    cube = jnp.einsum("jb,ijcm->ibcm", interp31, cube, precision=hi)
    cube = jnp.einsum("ia,ibcm->abcm", interp31, cube, precision=hi)
    return cube.reshape(8, width)


def prolong(coarse, interp31):
    hi = lax.Precision.HIGHEST
    width = coarse.shape[1]
    cube = coarse.reshape(2, 2, 2, width)
    cube = jnp.einsum("ck,ijkm->ijcm", interp31, cube, precision=hi)
    cube = jnp.einsum("bj,ijcm->ibcm", interp31, cube, precision=hi)
    cube = jnp.einsum("ai,ibcm->abcm", interp31, cube, precision=hi)
    return cube.reshape(64, width)


def assemble(values, conn_ids, count):
    layers = values.shape[0]
    flat = values.reshape(layers, -1).T
    summed = jax.ops.segment_sum(flat, conn_ids.reshape(-1), num_segments=count)
    return summed.T


def element_term(operators, conn_ids, field):
    return jnp.einsum("pqe,qe->pe", operators, field[conn_ids], precision=lax.Precision.HIGHEST)


def share(nodes, faces):
    lower = faces[0, 0]
    upper = faces[1, 0]
    planes = jnp.stack([nodes[:, lower], nodes[:, upper]], axis=1)
    padded = extended(planes, (("slab", 1),), 1)
    return nodes.at[:, lower].add(padded[:, 0]).at[:, upper].add(padded[:, 3])


def local(resid7, interp73, interp31, elem_ops, conn, faces):
    own = resid7.shape[1]
    slab_elems = conn.shape[1]
    layers = slab_elems // (EX * EY)
    count = (EX + 1) * (EY + 1) * (layers + 1)
    start = lax.axis_index("grp") * own
    own_conn = lax.dynamic_slice_in_dim(conn, start, own, 1)
    middle_res = restrict_high(resid7, interp73)
    blocks = lax.all_gather(middle_res, "grp", axis=1, tiled=True)
    slab_res = restrict_low(blocks, interp31)
    pair = jnp.stack([slab_res, jnp.einsum("ppe->pe", elem_ops)])
    both_nodes = assemble(pair, conn, count)
    shared = share(both_nodes, faces)
    rhs = shared[0]
    diag = shared[1]
    theta = 0.5 * (lam_high + lam_low)
    delta = 0.5 * (lam_high - lam_low)
    sigma = theta / delta
    inverse = 1.0 / diag
    direction = inverse * rhs / theta
    solution = direction
    remain = rhs
    rho = 1.0 / sigma
    for sweep in range(SWEEPS):
        nodes = assemble(element_term(elem_ops, conn, direction)[None], conn, count)
        remain = remain - share(nodes, faces)[0]
        rho_new = 1.0 / (2.0 * sigma - rho)
        direction = rho_new * rho * direction + 2.0 * rho_new / delta * inverse * remain
        solution = solution + direction
        rho = rho_new
    return prolong(solution[own_conn], interp31)


def solution(mesh):
    in_specs = (
        P(None, ("slab", "grp")),
        P(),
        P(),
        P(None, None, "slab"),
        P(None, "slab"),
        P(None, "slab", None),
    )
    out_specs = P(None, ("slab", "grp"))
    return jax.shard_map(local, mesh=mesh, in_specs=in_specs, out_specs=out_specs, check_vma=False)
```

profile of v0, /device:TPU:12, one launch (start us, length us, event | category | flops | bytes accessed | tf_op | source)
XLA Modules:
  0.0 223.9 jit_solution(7532873134520829746)
XLA Ops:
  0.0 0.8 copy.70
  0.8 1.0 select_reduce_fusion
  1.8 1.0 convolution_bitcast_fusion
  2.8 0.0 copy-start.2
  2.8 0.9 convolution_bitcast_fusion.2
  3.8 0.9 convolution_bitcast_fusion.5
  4.7 13.9 %all_gather.3 = f32[64,512]{1,0:T(8,128)S(1)} all-gather(f32[64,128]{1,0:T(8,128)S(1)} %bitcast.100), channel_id=1, replica_groups=mesh['slab'=8,'grp'=4] {'grp'}, dimensions={1}, use_global_device_ids=true | all-gather | bytes 163840 | tf_op jit(solution)/shard_map/all_gather | solution.py:83
  18.6 1.0 convolution_bitcast_fusion.1
  19.7 0.9 convolution_bitcast_fusion.4
  20.6 0.9 convolution_bitcast_fusion.7
  21.6 0.7 copy.46
  22.3 22.5 %scatter_custom_fusion = f32[1122,2]{1,0:T(8,128)S(1)} fusion(s32[4096]{0:T(1024)S(1)} %bitcast.109, f32[4096,2]{1,0:T(8,128)S(1)} %copy.46, f32[]{:T(128)} %constant.13.clone.1), kind=kCustom, calls=%fused_computation.31 | custom fusion | flops 8192 | bytes 8980 | tf_op jit(solution)/shard_map/scatter-add | solution.py:59
  44.8 1.6 gather_fusion
  46.4 1.9 collective-permute-start
  48.3 1.6 gather_fusion.1
  49.9 4.5 %collective-permute-start.1 = (f32[2,1,561]{0,2,1:T(8,128)S(1)}, f32[2,1,561]{0,2,1:T(8,128)S(1)}, u32[]{:S(2)}, u32[]{:S(2)}) collective-permute-start(f32[2,1,561]{0,2,1:T(8,128)S(1)} %bitcast.115), channel_id=1, source_target_pairs={{4,0},{8,4},{12,8},{16,12},{20,16},{24,20},{28,24},{5,1},{9,5},{13... | collective-permute-start | bytes 13472 | tf_op jit(solution)/shard_map/ppermute | solution.py:21
  54.5 0.7 collective-permute-done
  55.3 6.4 %scatter_custom_fusion.1 = f32[2,1122]{0,1:T(8,128)S(1)} fusion(f32[2,1122]{0,1:T(8,128)S(1)} %bitcast.99, s32[561]{0:T(1024)S(1)} %get-tuple-element.6, f32[2,1,561]{0,2,1:T(8,128)S(1)} %collective-permute-done), kind=kCustom, calls=%fused_computation.29 | custom fusion | flops 1122 | bytes 299792 | tf_op jit(solution)/shard_map/scatter-add | solution.py:72
  61.7 0.0 collective-permute-done.1
  61.7 6.4 %scatter_custom_fusion.2 = f32[2,1122]{0,1:T(8,128)S(1)} fusion(f32[2,1122]{0,1:T(8,128)S(1)} %scatter_custom_fusion.1, s32[561]{0:T(1024)S(1)} %get-tuple-element.5, f32[2,1,561]{0,2,1:T(8,128)S(1)} %collective-permute-done.1), kind=kCustom, calls=%fused_computation.27 | custom fusion | flops 1122 | bytes 299792 | tf_op jit(solution)/shard_map/scatter-add | solution.py:72
  68.1 0.2 fusion.32
  68.3 0.2 copy.67
  68.5 0.2 copy.66
  68.8 0.1 multiply_reduce_fusion.2
  68.8 0.0 copy-start.1
  68.8 23.0 %gather_fusion.2 = f32[4096]{0:T(1024)S(1)} fusion(f32[1122]{0:T(1024)S(1)} %get-tuple-element.7, s32[4096]{0:T(1024)S(1)} %broadcast_clamp_fusion), kind=kCustom, calls=%fused_computation.2 | custom fusion | bytes 49152 | tf_op jit(solution)/shard_map/gather | solution.py:64
  92.0 26.4 %scatter_custom_fusion.3 = f32[1122]{0:T(1024)S(1)} fusion(s32[4096]{0:T(1024)S(1)} %bitcast.110, f32[4096]{0:T(1024)S(1)} %bitcast.113, f32[]{:T(128)} %constant.13.clone.1), kind=kCustom, calls=%fused_computation.62 | custom fusion | flops 4096 | bytes 4492 | tf_op jit(solution)/shard_map/scatter-add | solution.py:59
  118.4 3.6 %gather_fusion.3 = f32[561]{0:T(1024)S(1)} fusion(f32[1122]{0:T(1024)S(1)} %scatter_custom_fusion.3, s32[1024]{0:T(1024)S(1)} %get-tuple-element.12), kind=kCustom, calls=%fused_computation.3 | custom fusion | bytes 6732 | tf_op jit(solution)/shard_map/gather | solution.py:70
  122.0 2.1 collective-permute-start.2
  124.1 3.6 %gather_fusion.4 = f32[561]{0:T(1024)S(1)} fusion(f32[1122]{0:T(1024)S(1)} %scatter_custom_fusion.3, s32[1024]{0:T(1024)S(1)} %get-tuple-element.11), kind=kCustom, calls=%fused_computation.4 | custom fusion | bytes 6732 | tf_op jit(solution)/shard_map/gather | solution.py:70
  127.7 4.4 %collective-permute-start.3 = (f32[1,1,561]{2,1,0:T(1,128)S(1)}, f32[1,1,561]{2,1,0:T(1,128)S(1)}, u32[]{:S(2)}, u32[]{:S(2)}) collective-permute-start(f32[1,1,561]{2,1,0:T(1,128)S(1)} %stack.32), channel_id=1, source_target_pairs={{4,0},{8,4},{12,8},{16,12},{20,16},{24,20},{28,24},{5,1},{9,5},{13... | collective-permute-start | bytes 6740 | tf_op jit(solution)/shard_map/ppermute | solution.py:21
  132.0 0.0 collective-permute-done.2
  132.1 5.3 %scatter_fusion = f32[1122]{0:T(1024)S(1)} fusion(f32[1122]{0:T(1024)S(1)} %scatter_custom_fusion.3, s32[561]{0:T(1024)S(1)} %get-tuple-element.6, f32[561]{0:T(1024)S(1)} %reduce.5), kind=kCustom, calls=%fused_computation.13 | custom fusion | flops 561 | bytes 8976 | tf_op jit(solution)/shard_map/scatter-add | solution.py:72
  137.4 5.2 %scatter_fusion.1 = f32[1122]{0:T(1024)S(1)} fusion(f32[1122]{0:T(1024)S(1)} %scatter_fusion, s32[561]{0:T(1024)S(1)} %get-tuple-element.5, f32[561]{0:T(1024)S(1)} %reduce.6), kind=kCustom, calls=%fused_computation.14 | custom fusion | flops 561 | bytes 8976 | tf_op jit(solution)/shard_map/scatter-add | solution.py:72
  142.6 23.0 %gather_fusion.5 = f32[4096]{0:T(1024)S(1)} fusion(f32[1122]{0:T(1024)S(1)} %add_reduce_fusion, s32[4096]{0:T(1024)S(1)} %broadcast_clamp_fusion), kind=kCustom, calls=%fused_computation.5 | custom fusion | bytes 49152 | tf_op jit(solution)/shard_map/gather | solution.py:64
  165.7 26.4 %scatter_custom_fusion.6 = f32[1122]{0:T(1024)S(1)} fusion(s32[4096]{0:T(1024)S(1)} %bitcast.111, f32[4096]{0:T(1024)S(1)} %bitcast.112, f32[]{:T(128)} %constant.13.clone.1), kind=kCustom, calls=%fused_computation.60 | custom fusion | flops 4096 | bytes 4492 | tf_op jit(solution)/shard_map/scatter-add | solution.py:59
  192.2 3.6 %gather_fusion.7 = f32[561]{0:T(1024)S(1)} fusion(f32[1122]{0:T(1024)S(1)} %scatter_custom_fusion.6, s32[1024]{0:T(1024)S(1)} %get-tuple-element.11), kind=kCustom, calls=%fused_computation.7 | custom fusion | bytes 6732 | tf_op jit(solution)/shard_map/gather | solution.py:70
  195.7 3.6 %gather_fusion.6 = f32[561]{0:T(1024)S(1)} fusion(f32[1122]{0:T(1024)S(1)} %scatter_custom_fusion.6, s32[1024]{0:T(1024)S(1)} %get-tuple-element.12), kind=kCustom, calls=%fused_computation.6 | custom fusion | bytes 6732 | tf_op jit(solution)/shard_map/gather | solution.py:70
  199.3 1.9 collective-permute-start.4
  201.2 4.5 %collective-permute-start.5 = (f32[1,1,561]{2,1,0:T(1,128)S(1)}, f32[1,1,561]{2,1,0:T(1,128)S(1)}, u32[]{:S(2)}, u32[]{:S(2)}) collective-permute-start(f32[1,1,561]{2,1,0:T(1,128)S(1)} %stack.34), channel_id=1, source_target_pairs={{4,0},{8,4},{12,8},{16,12},{20,16},{24,20},{28,24},{5,1},{9,5},{13... | collective-permute-start | bytes 6740 | tf_op jit(solution)/shard_map/ppermute | solution.py:21
  205.8 5.3 %scatter_fusion.2 = f32[1122]{0:T(1024)S(1)} fusion(f32[1122]{0:T(1024)S(1)} %scatter_custom_fusion.6, s32[561]{0:T(1024)S(1)} %get-tuple-element.6, f32[561]{0:T(1024)S(1)} %reduce.8), kind=kCustom, calls=%fused_computation.16 | custom fusion | flops 561 | bytes 8976 | tf_op jit(solution)/shard_map/scatter-add | solution.py:72
  211.2 5.2 %scatter_fusion.3 = f32[1122]{0:T(1024)S(1)} fusion(f32[1122]{0:T(1024)S(1)} %scatter_fusion.2, s32[561]{0:T(1024)S(1)} %get-tuple-element.5, f32[561]{0:T(1024)S(1)} %reduce.9), kind=kCustom, calls=%fused_computation.17 | custom fusion | flops 561 | bytes 8976 | tf_op jit(solution)/shard_map/scatter-add | solution.py:72
  216.4 0.0 copy-start.3
  216.4 6.2 %gather_fusion.8 = f32[1024]{0:T(1024)S(1)} fusion(f32[1122]{0:T(1024)S(1)} %add_add_fusion, s32[1024]{0:T(1024)S(1)} %fusion.16), kind=kCustom, calls=%fused_computation.8 | custom fusion | bytes 12288 | tf_op jit(solution)/shard_map/gather | solution.py:105
  222.6 0.2 convolution_bitcast_fusion.8
  222.8 0.2 convolution_bitcast_fusion.6
  223.0 0.3 convolution_bitcast_fusion.3
  223.3 0.6 copy.51
  (40 shorter events, 0.5 us)
Async XLA Ops:
  0.0 1.8 copy-start
  0.0 22.2 %copy-start.4 = (s32[2,1,561]{2,1,0:T(1,128)S(1)}, s32[2,1,561]{2,1,0:T(1,128)}, u32[]{:S(2)}) copy-start(s32[2,1,561]{2,1,0:T(1,128)} %param.11) | copy-start | bytes 13468
  2.8 51.7 %copy-start.2 = (s32[8,512]{1,0:T(8,128)S(1)}, s32[8,512]{1,0:T(8,128)}, u32[]{:S(2)}) copy-start(s32[8,512]{1,0:T(8,128)} %param.10) | copy-start | bytes 49156
  46.4 8.9 %collective-permute-start = (f32[2,1,561]{0,2,1:T(8,128)S(1)}, f32[2,1,561]{0,2,1:T(8,128)S(1)}, u32[]{:S(2)}, u32[]{:S(2)}) collective-permute-start(f32[2,1,561]{0,2,1:T(8,128)S(1)} %bitcast.116), channel_id=1, source_target_pairs={{0,4},{4,8},{8,12},{12,16},{16,20},{20,24},{24,28},{1,5},{5,9},{9,... | collective-permute-start | bytes 13472 | tf_op jit(solution)/shard_map/ppermute | solution.py:20
  49.9 11.7 %collective-permute-start.1 = (f32[2,1,561]{0,2,1:T(8,128)S(1)}, f32[2,1,561]{0,2,1:T(8,128)S(1)}, u32[]{:S(2)}, u32[]{:S(2)}) collective-permute-start(f32[2,1,561]{0,2,1:T(8,128)S(1)} %bitcast.115), channel_id=1, source_target_pairs={{4,0},{8,4},{12,8},{16,12},{20,16},{24,20},{28,24},{5,1},{9,5},{13... | collective-permute-start | bytes 13472 | tf_op jit(solution)/shard_map/ppermute | solution.py:21
  68.8 23.1 %copy-start.1 = (f32[8,8,512]{2,1,0:T(8,128)S(1)}, f32[8,8,512]{2,1,0:T(8,128)}, u32[]{:S(2)}) copy-start(f32[8,8,512]{2,1,0:T(8,128)} %param.9) | copy-start | bytes 393220
  122.0 10.1 %collective-permute-start.2 = (f32[1,1,561]{2,1,0:T(1,128)S(1)}, f32[1,1,561]{2,1,0:T(1,128)S(1)}, u32[]{:S(2)}, u32[]{:S(2)}) collective-permute-start(f32[1,1,561]{2,1,0:T(1,128)S(1)} %stack.31), channel_id=1, source_target_pairs={{0,4},{4,8},{8,12},{12,16},{16,20},{20,24},{24,28},{1,5},{5,9},{9,... | collective-permute-start | bytes 6740 | tf_op jit(solution)/shard_map/ppermute | solution.py:20
  127.7 9.7 %collective-permute-start.3 = (f32[1,1,561]{2,1,0:T(1,128)S(1)}, f32[1,1,561]{2,1,0:T(1,128)S(1)}, u32[]{:S(2)}, u32[]{:S(2)}) collective-permute-start(f32[1,1,561]{2,1,0:T(1,128)S(1)} %stack.32), channel_id=1, source_target_pairs={{4,0},{8,4},{12,8},{16,12},{20,16},{24,20},{28,24},{5,1},{9,5},{13... | collective-permute-start | bytes 6740 | tf_op jit(solution)/shard_map/ppermute | solution.py:21
  199.3 6.5 %collective-permute-start.4 = (f32[1,1,561]{2,1,0:T(1,128)S(1)}, f32[1,1,561]{2,1,0:T(1,128)S(1)}, u32[]{:S(2)}, u32[]{:S(2)}) collective-permute-start(f32[1,1,561]{2,1,0:T(1,128)S(1)} %stack.33), channel_id=1, source_target_pairs={{0,4},{4,8},{8,12},{12,16},{16,20},{20,24},{24,28},{1,5},{5,9},{9,... | collective-permute-start | bytes 6740 | tf_op jit(solution)/shard_map/ppermute | solution.py:20
  201.2 9.9 %collective-permute-start.5 = (f32[1,1,561]{2,1,0:T(1,128)S(1)}, f32[1,1,561]{2,1,0:T(1,128)S(1)}, u32[]{:S(2)}, u32[]{:S(2)}) collective-permute-start(f32[1,1,561]{2,1,0:T(1,128)S(1)} %stack.34), channel_id=1, source_target_pairs={{4,0},{8,4},{12,8},{16,12},{20,16},{24,20},{28,24},{5,1},{9,5},{13... | collective-permute-start | bytes 6740 | tf_op jit(solution)/shard_map/ppermute | solution.py:21
  216.4 6.2 %copy-start.3 = (f32[4,2]{0,1:T(2,128)S(1)}, f32[4,2]{0,1:T(2,128)}, u32[]{:S(2)}) copy-start(f32[4,2]{0,1:T(2,128)} %param.8) | copy-start | bytes 100
where the time goes:
time: 224 us
  other arithmetic  110 us (49%)
  local copies, waits for them, and re-layouts  72.5 us (32%)
  starting transfers between devices  19.4 us (9%)
  blocking collectives  13.9 us (6%)
  matrix products  6.36 us (3%)
    scatter-add x3, other arithmetic, assemble(): summed = jax.ops.segment_sum(flat, conn_ids.reshape(-1), num_segments=count)  75.3 us
    gather x4, local copies, waits for them, and re-layouts, element_term(): field[conn_ids]  46.1 us
    scatter-add x6, other arithmetic, share(): return nodes.at[:, lower].add(padded[:, 0]).at[:, upper].add(padded[:, 3])  33.7 us
    gather x6, local copies, waits for them, and re-layouts, share(): planes = jnp.stack([nodes[:, lower], nodes[:, upper]], axis=1)  17.5 us
    all_gather x1, blocking collectives, local(): blocks = lax.all_gather(middle_res, 'grp', axis=1, tiled=True)  13.9 us
    ppermute x3, starting transfers between devices, extended(): after = lax.ppermute(first, axis, down)  13.4 us
    gather x1, local copies, waits for them, and re-layouts, local(): return prolong(solution[own_conn], interp31)  6.15 us
    ppermute x3, starting transfers between devices, extended(): before = lax.ppermute(last, axis, up)  5.94 us
  transfers between devices with their start and end apart: 6, of which 1 were waited for; matrix products, arithmetic and copies ran while one was open for 10% of the time, Pallas kernels for 0%

commit v1 on v0

--- a/solution.py
+++ b/solution.py
@@ -8,6 +8,18 @@
 SWEEPS = 2
 lam_low = 0.3
 lam_high = 1.9
+
+
+def collect(array, axis, dim):
+    ways, here, step = (lax.axis_size(axis), lax.axis_index(axis), array.shape[dim])
+    line, have = (array, 1)
+    while have < ways:
+        line = jnp.concatenate(
+            [line, lax.ppermute(line, axis, [(d, (d - have) % ways) for d in range(ways)])],
+            axis=dim,
+        )
+        have = 2 * have
+    return jnp.roll(line, here * step, axis=dim)
 
 
 def extended(array, sides, width):
@@ -80,7 +92,7 @@
     start = lax.axis_index("grp") * own
     own_conn = lax.dynamic_slice_in_dim(conn, start, own, 1)
     middle_res = restrict_high(resid7, interp73)
-    blocks = lax.all_gather(middle_res, "grp", axis=1, tiled=True)
+    blocks = collect(middle_res, "grp", 1)
     slab_res = restrict_low(blocks, interp31)
     pair = jnp.stack([slab_res, jnp.einsum("ppe->pe", elem_ops)])
     both_nodes = assemble(pair, conn, count)

time: 224 us -> 221 us (0.987); the launches traced: 224 us -> 219 us
  blocking collectives: 13.9 us -> 0 us
  starting transfers between devices: 19.4 us -> 24.3 us
  other arithmetic: 110 us -> 113 us
  waiting for transfers between devices: 0.76 us -> 3.26 us
    all_gather x1 -> x0, blocking collectives: 13.9 us -> none  [local(): blocks = lax.all_gather(middle_res, 'grp', axis=1, tiled=True)]
    ppermute x0 -> x2, starting transfers between devices: none -> 4.89 us  [collect(): lax.ppermute(line, axis, [(d, (d - have) % ways) for d in range(ways)])]
    ppermute x0 -> x2, waiting for transfers between devices: none -> 2.46 us  [collect(): lax.ppermute(line, axis, [(d, (d - have) % ways) for d in range(ways)])]
  transfers between devices with their start and end apart: 6 -> 8, of which waited for: 1 -> 3; matrix products, arithmetic and copies ran while one was open for 10% -> 12% of each run, Pallas kernels for 0% -> 0%
where the time goes in v1:
time: 221 us; the launch traced here: 219 us
  other arithmetic  113 us (51%)
  local copies, waits for them, and re-layouts  73.5 us (33%)
  starting transfers between devices  24.3 us (11%)
  matrix products  4.33 us (2%)
  waiting for transfers between devices  3.26 us (1%)
    scatter-add x3, other arithmetic, assemble(): summed = jax.ops.segment_sum(flat, conn_ids.reshape(-1), num_segments=count)  75.5 us
    gather x4, local copies, waits for them, and re-layouts, element_term(): field[conn_ids]  46.1 us
    scatter-add x6, other arithmetic, share(): return nodes.at[:, lower].add(padded[:, 0]).at[:, upper].add(padded[:, 3])  33.7 us
    gather x6, local copies, waits for them, and re-layouts, share(): planes = jnp.stack([nodes[:, lower], nodes[:, upper]], axis=1)  17.5 us
    ppermute x3, starting transfers between devices, extended(): after = lax.ppermute(first, axis, down)  13.6 us
    gather x1, local copies, waits for them, and re-layouts, local(): return prolong(solution[own_conn], interp31)  6.15 us
    ppermute x3, starting transfers between devices, extended(): before = lax.ppermute(last, axis, up)  5.76 us
    ppermute x2, starting transfers between devices, collect(): lax.ppermute(line, axis, [(d, (d - have) % ways) for d in range(ways)])  4.89 us
  transfers between devices with their start and end apart: 8, of which 3 were waited for; matrix products, arithmetic and copies ran while one was open for 12% of the time, Pallas kernels for 0%

profile of v1, /device:TPU:12, one launch (start us, length us, event | category | flops | bytes accessed | tf_op | source)
XLA Modules:
  0.0 218.6 jit_solution(14681502068480602413)
XLA Ops:
  0.0 0.9 copy-done
  1.0 1.0 convolution_bitcast_fusion
  2.0 0.9 convolution_bitcast_fusion.2
  2.9 0.9 convolution_bitcast_fusion.5
  3.8 0.5 collective-permute-start
  4.4 0.7 fusion.22
  5.1 0.7 fusion.10
  5.8 1.0 select_reduce_fusion
  6.9 0.7 copy.70
  7.6 0.2 collective-permute-done
  7.8 4.4 %collective-permute-start.1 = (f32[64,256]{1,0:T(8,128)S(1)}, f32[64,256]{1,0:T(8,128)S(1)}, u32[]{:S(2)}, u32[]{:S(2)}) collective-permute-start(f32[64,256]{1,0:T(8,128)S(1)} %pad_maximum_fusion), channel_id=1, source_target_pairs={{0,2},{1,3},{2,0},{3,1},{4,6},{5,7},{6,4},{7,5},{8,10},{9,11},{10,... | collective-permute-start | bytes 196616 | tf_op jit(solution)/shard_map/ppermute | solution.py:18
  12.2 2.2 %collective-permute-done.1 = f32[64,256]{1,0:T(8,128)S(1)} collective-permute-done((f32[64,256]{1,0:T(8,128)S(1)}, f32[64,256]{1,0:T(8,128)S(1)}, u32[]{:S(2)}, u32[]{:S(2)}) %collective-permute-start.1) | collective-permute-done | bytes 65568 | tf_op jit(solution)/shard_map/ppermute | solution.py:18
  14.6 0.3 convolution_bitcast_fusion.1
  14.9 0.3 convolution_bitcast_fusion.4
  15.5 0.7 copy.46
  16.1 22.5 %scatter_custom_fusion = f32[1122,2]{1,0:T(8,128)S(1)} fusion(s32[4096]{0:T(1024)S(1)} %bitcast.112, f32[4096,2]{1,0:T(8,128)S(1)} %copy.46, f32[]{:T(128)} %constant.17.clone.1), kind=kCustom, calls=%fused_computation.31 | custom fusion | flops 8192 | bytes 8980 | tf_op jit(solution)/shard_map/scatter-add | solution.py:71
  38.6 1.6 gather_fusion
  40.3 1.9 collective-permute-start.2
  42.2 1.6 gather_fusion.1
  43.8 4.5 %collective-permute-start.3 = (f32[2,1,561]{0,2,1:T(8,128)S(1)}, f32[2,1,561]{0,2,1:T(8,128)S(1)}, u32[]{:S(2)}, u32[]{:S(2)}) collective-permute-start(f32[2,1,561]{0,2,1:T(8,128)S(1)} %bitcast.118), channel_id=1, source_target_pairs={{4,0},{8,4},{12,8},{16,12},{20,16},{24,20},{28,24},{5,1},{9,5},{13... | collective-permute-start | bytes 13472 | tf_op jit(solution)/shard_map/ppermute | solution.py:33
  48.4 0.8 collective-permute-done.2
  49.2 6.4 %scatter_custom_fusion.1 = f32[2,1122]{0,1:T(8,128)S(1)} fusion(f32[2,1122]{0,1:T(8,128)S(1)} %bitcast.99, s32[561]{0:T(1024)S(1)} %get-tuple-element.6, f32[2,1,561]{0,2,1:T(8,128)S(1)} %collective-permute-done.2), kind=kCustom, calls=%fused_computation.29 | custom fusion | flops 1122 | bytes 299792 | tf_op jit(solution)/shard_map/scatter-add | solution.py:84
  55.6 6.4 %scatter_custom_fusion.2 = f32[2,1122]{0,1:T(8,128)S(1)} fusion(f32[2,1122]{0,1:T(8,128)S(1)} %scatter_custom_fusion.1, s32[561]{0:T(1024)S(1)} %get-tuple-element.5, f32[2,1,561]{0,2,1:T(8,128)S(1)} %collective-permute-done.3), kind=kCustom, calls=%fused_computation.27 | custom fusion | flops 1122 | bytes 299792 | tf_op jit(solution)/shard_map/scatter-add | solution.py:84
  62.0 0.2 fusion.32
  62.2 0.2 copy.66
  62.4 0.2 copy.67
  62.7 23.0 %gather_fusion.2 = f32[4096]{0:T(1024)S(1)} fusion(f32[1122]{0:T(1024)S(1)} %get-tuple-element.7, s32[4096]{0:T(1024)S(1)} %broadcast_clamp_fusion), kind=kCustom, calls=%fused_computation.2 | custom fusion | bytes 49152 | tf_op jit(solution)/shard_map/gather | solution.py:76
  85.8 26.6 %scatter_custom_fusion.3 = f32[1122]{0:T(1024)S(1)} fusion(s32[4096]{0:T(1024)S(1)} %bitcast.113, f32[4096]{0:T(1024)S(1)} %bitcast.116, f32[]{:T(128)} %constant.17.clone.1), kind=kCustom, calls=%fused_computation.69 | custom fusion | flops 4096 | bytes 4492 | tf_op jit(solution)/shard_map/scatter-add | solution.py:71
  112.4 3.6 %gather_fusion.3 = f32[561]{0:T(1024)S(1)} fusion(f32[1122]{0:T(1024)S(1)} %scatter_custom_fusion.3, s32[1024]{0:T(1024)S(1)} %get-tuple-element.12), kind=kCustom, calls=%fused_computation.3 | custom fusion | bytes 6732 | tf_op jit(solution)/shard_map/gather | solution.py:82
  116.0 1.9 collective-permute-start.4
  117.9 3.6 %gather_fusion.4 = f32[561]{0:T(1024)S(1)} fusion(f32[1122]{0:T(1024)S(1)} %scatter_custom_fusion.3, s32[1024]{0:T(1024)S(1)} %get-tuple-element.11), kind=kCustom, calls=%fused_computation.4 | custom fusion | bytes 6732 | tf_op jit(solution)/shard_map/gather | solution.py:82
  121.5 4.5 %collective-permute-start.5 = (f32[1,1,561]{2,1,0:T(1,128)S(1)}, f32[1,1,561]{2,1,0:T(1,128)S(1)}, u32[]{:S(2)}, u32[]{:S(2)}) collective-permute-start(f32[1,1,561]{2,1,0:T(1,128)S(1)} %stack.32), channel_id=1, source_target_pairs={{4,0},{8,4},{12,8},{16,12},{20,16},{24,20},{28,24},{5,1},{9,5},{13... | collective-permute-start | bytes 6740 | tf_op jit(solution)/shard_map/ppermute | solution.py:33
  126.1 5.3 %scatter_fusion = f32[1122]{0:T(1024)S(1)} fusion(f32[1122]{0:T(1024)S(1)} %scatter_custom_fusion.3, s32[561]{0:T(1024)S(1)} %get-tuple-element.6, f32[561]{0:T(1024)S(1)} %reduce.5), kind=kCustom, calls=%fused_computation.13 | custom fusion | flops 561 | bytes 8976 | tf_op jit(solution)/shard_map/scatter-add | solution.py:84
  131.4 5.2 %scatter_fusion.1 = f32[1122]{0:T(1024)S(1)} fusion(f32[1122]{0:T(1024)S(1)} %scatter_fusion, s32[561]{0:T(1024)S(1)} %get-tuple-element.5, f32[561]{0:T(1024)S(1)} %reduce.6), kind=kCustom, calls=%fused_computation.14 | custom fusion | flops 561 | bytes 8976 | tf_op jit(solution)/shard_map/scatter-add | solution.py:84
  136.6 23.0 %gather_fusion.5 = f32[4096]{0:T(1024)S(1)} fusion(f32[1122]{0:T(1024)S(1)} %add_reduce_fusion, s32[4096]{0:T(1024)S(1)} %broadcast_clamp_fusion), kind=kCustom, calls=%fused_computation.5 | custom fusion | bytes 49152 | tf_op jit(solution)/shard_map/gather | solution.py:76
  159.8 26.4 %scatter_custom_fusion.6 = f32[1122]{0:T(1024)S(1)} fusion(s32[4096]{0:T(1024)S(1)} %bitcast.114, f32[4096]{0:T(1024)S(1)} %bitcast.115, f32[]{:T(128)} %constant.17.clone.1), kind=kCustom, calls=%fused_computation.67 | custom fusion | flops 4096 | bytes 4492 | tf_op jit(solution)/shard_map/scatter-add | solution.py:71
  186.2 3.6 %gather_fusion.6 = f32[561]{0:T(1024)S(1)} fusion(f32[1122]{0:T(1024)S(1)} %scatter_custom_fusion.6, s32[1024]{0:T(1024)S(1)} %get-tuple-element.12), kind=kCustom, calls=%fused_computation.6 | custom fusion | bytes 6732 | tf_op jit(solution)/shard_map/gather | solution.py:82
  189.8 3.6 %gather_fusion.7 = f32[561]{0:T(1024)S(1)} fusion(f32[1122]{0:T(1024)S(1)} %scatter_custom_fusion.6, s32[1024]{0:T(1024)S(1)} %get-tuple-element.11), kind=kCustom, calls=%fused_computation.7 | custom fusion | bytes 6732 | tf_op jit(solution)/shard_map/gather | solution.py:82
  193.3 1.9 collective-permute-start.6
  195.3 4.5 %collective-permute-start.7 = (f32[1,1,561]{2,1,0:T(1,128)S(1)}, f32[1,1,561]{2,1,0:T(1,128)S(1)}, u32[]{:S(2)}, u32[]{:S(2)}) collective-permute-start(f32[1,1,561]{2,1,0:T(1,128)S(1)} %stack.34), channel_id=1, source_target_pairs={{4,0},{8,4},{12,8},{16,12},{20,16},{24,20},{28,24},{5,1},{9,5},{13... | collective-permute-start | bytes 6740 | tf_op jit(solution)/shard_map/ppermute | solution.py:33
  199.8 0.7 fusion.16
  200.6 5.3 %scatter_fusion.2 = f32[1122]{0:T(1024)S(1)} fusion(f32[1122]{0:T(1024)S(1)} %scatter_custom_fusion.6, s32[561]{0:T(1024)S(1)} %get-tuple-element.6, f32[561]{0:T(1024)S(1)} %reduce.8), kind=kCustom, calls=%fused_computation.16 | custom fusion | flops 561 | bytes 8976 | tf_op jit(solution)/shard_map/scatter-add | solution.py:84
  205.9 5.2 %scatter_fusion.3 = f32[1122]{0:T(1024)S(1)} fusion(f32[1122]{0:T(1024)S(1)} %scatter_fusion.2, s32[561]{0:T(1024)S(1)} %get-tuple-element.5, f32[561]{0:T(1024)S(1)} %reduce.9), kind=kCustom, calls=%fused_computation.17 | custom fusion | flops 561 | bytes 8976 | tf_op jit(solution)/shard_map/scatter-add | solution.py:84
  211.1 6.2 %gather_fusion.8 = f32[1024]{0:T(1024)S(1)} fusion(f32[1122]{0:T(1024)S(1)} %add_add_fusion, s32[1024]{0:T(1024)S(1)} %fusion.16), kind=kCustom, calls=%fused_computation.8 | custom fusion | bytes 12288 | tf_op jit(solution)/shard_map/gather | solution.py:117
  217.3 0.2 convolution_bitcast_fusion.8
  217.5 0.2 convolution_bitcast_fusion.6
  217.7 0.3 convolution_bitcast_fusion.3
  218.0 0.6 copy.51
  (47 shorter events, 0.7 us)
Async XLA Ops:
  0.0 1.0 copy-start
  1.0 13.6 %copy-start.2 = (f32[4,2]{0,1:T(2,128)S(1)}, f32[4,2]{0,1:T(2,128)}, u32[]{:S(2)}) copy-start(f32[4,2]{0,1:T(2,128)} %param.8) | copy-start | bytes 100
  3.8 4.0 %collective-permute-start = (f32[64,128]{1,0:T(8,128)S(1)}, f32[64,128]{1,0:T(8,128)S(1)}, u32[]{:S(2)}, u32[]{:S(2)}) collective-permute-start(f32[64,128]{1,0:T(8,128)S(1)} %bitcast.100), channel_id=1, source_target_pairs={{0,3},{1,0},{2,1},{3,2},{4,7},{5,4},{6,5},{7,6},{8,11},{9,8},{10,9... | collective-permute-start | bytes 98312 | tf_op jit(solution)/shard_map/ppermute | solution.py:18
  7.8 6.6 %collective-permute-start.1 = (f32[64,256]{1,0:T(8,128)S(1)}, f32[64,256]{1,0:T(8,128)S(1)}, u32[]{:S(2)}, u32[]{:S(2)}) collective-permute-start(f32[64,256]{1,0:T(8,128)S(1)} %pad_maximum_fusion), channel_id=1, source_target_pairs={{0,2},{1,3},{2,0},{3,1},{4,6},{5,7},{6,4},{7,5},{8,10},{9,11},{10,... | collective-permute-start | bytes 196616 | tf_op jit(solution)/shard_map/ppermute | solution.py:18
  40.3 8.9 %collective-permute-start.2 = (f32[2,1,561]{0,2,1:T(8,128)S(1)}, f32[2,1,561]{0,2,1:T(8,128)S(1)}, u32[]{:S(2)}, u32[]{:S(2)}) collective-permute-start(f32[2,1,561]{0,2,1:T(8,128)S(1)} %bitcast.119), channel_id=1, source_target_pairs={{0,4},{4,8},{8,12},{12,16},{16,20},{20,24},{24,28},{1,5},{5,9},{9,... | collective-permute-start | bytes 13472 | tf_op jit(solution)/shard_map/ppermute | solution.py:32
  43.8 11.7 %collective-permute-start.3 = (f32[2,1,561]{0,2,1:T(8,128)S(1)}, f32[2,1,561]{0,2,1:T(8,128)S(1)}, u32[]{:S(2)}, u32[]{:S(2)}) collective-permute-start(f32[2,1,561]{0,2,1:T(8,128)S(1)} %bitcast.118), channel_id=1, source_target_pairs={{4,0},{8,4},{12,8},{16,12},{20,16},{24,20},{28,24},{5,1},{9,5},{13... | collective-permute-start | bytes 13472 | tf_op jit(solution)/shard_map/ppermute | solution.py:33
  62.7 23.1 %copy-start.1 = (f32[8,8,512]{2,1,0:T(8,128)S(1)}, f32[8,8,512]{2,1,0:T(8,128)}, u32[]{:S(2)}) copy-start(f32[8,8,512]{2,1,0:T(8,128)} %param.9) | copy-start | bytes 393220
  116.0 10.1 %collective-permute-start.4 = (f32[1,1,561]{2,1,0:T(1,128)S(1)}, f32[1,1,561]{2,1,0:T(1,128)S(1)}, u32[]{:S(2)}, u32[]{:S(2)}) collective-permute-start(f32[1,1,561]{2,1,0:T(1,128)S(1)} %stack.31), channel_id=1, source_target_pairs={{0,4},{4,8},{8,12},{12,16},{16,20},{20,24},{24,28},{1,5},{5,9},{9,... | collective-permute-start | bytes 6740 | tf_op jit(solution)/shard_map/ppermute | solution.py:32
  121.5 9.9 %collective-permute-start.5 = (f32[1,1,561]{2,1,0:T(1,128)S(1)}, f32[1,1,561]{2,1,0:T(1,128)S(1)}, u32[]{:S(2)}, u32[]{:S(2)}) collective-permute-start(f32[1,1,561]{2,1,0:T(1,128)S(1)} %stack.32), channel_id=1, source_target_pairs={{4,0},{8,4},{12,8},{16,12},{20,16},{24,20},{28,24},{5,1},{9,5},{13... | collective-permute-start | bytes 6740 | tf_op jit(solution)/shard_map/ppermute | solution.py:33
  193.3 7.2 %collective-permute-start.6 = (f32[1,1,561]{2,1,0:T(1,128)S(1)}, f32[1,1,561]{2,1,0:T(1,128)S(1)}, u32[]{:S(2)}, u32[]{:S(2)}) collective-permute-start(f32[1,1,561]{2,1,0:T(1,128)S(1)} %stack.33), channel_id=1, source_target_pairs={{0,4},{4,8},{8,12},{12,16},{16,20},{20,24},{24,28},{1,5},{5,9},{9,... | collective-permute-start | bytes 6740 | tf_op jit(solution)/shard_map/ppermute | solution.py:32
  195.3 10.5 %collective-permute-start.7 = (f32[1,1,561]{2,1,0:T(1,128)S(1)}, f32[1,1,561]{2,1,0:T(1,128)S(1)}, u32[]{:S(2)}, u32[]{:S(2)}) collective-permute-start(f32[1,1,561]{2,1,0:T(1,128)S(1)} %stack.34), channel_id=1, source_target_pairs={{4,0},{8,4},{12,8},{16,12},{20,16},{24,20},{28,24},{5,1},{9,5},{13... | collective-permute-start | bytes 6740 | tf_op jit(solution)/shard_map/ppermute | solution.py:33
